TPU v7x, 32 devices: a whole 2x2x4 slice. The times are simulated.
32 devices in a mesh: dp: 8 (over y, x, core), ctx: 4 (over z).
Axes of the slice: x: 2, y: 2, z: 4, core: 2. Of those that a mesh axis runs over, the one named last changes fastest.
Arguments:
- queries: bfloat16 [16384, 512], P(('dp', 'ctx')), parts along dimension 0, may hold values from -60 to 60
- key_vectors: bfloat16 [16384, 128], P(('dp', 'ctx')), parts along dimension 0, may hold values from -20 to 20
- value_vectors: bfloat16 [16384, 128], P(('dp', 'ctx')), parts along dimension 0, may hold values from -6 to 6
- block_plan: int32 [64], P('dp'), parts along dimension 0, may hold values from 0 to 7, each once
- doc_lengths: int32 [64], P('dp'), parts along dimension 0, may hold values from 1 to 1024, 2048 in all
- out_weight: bfloat16 [512, 4096], P(None, 'ctx'), may hold values from -0.25 to 0.25
Outputs:
- output: bfloat16 [16384, 4096], P(('dp', 'ctx')), parts along dimension 0
There are 8 independent parts, one for each index of `dp`. A program takes and returns all parts, laid end to end along the dimension named above; an argument that names none is the same for every part. Nothing has to cross between parts.
Inputs may be any that keep to these rules, and one draw needn't show every extreme that they name: `doc_lengths`: the 8 lengths sum to 2048.
All inputs are finite; a program needn't handle non-finite values.
Results may differ from a plain program's by a relative error of at most 0.013.
Values may be sent and summed in bfloat16 or wider, within the bound.
No kernel may reach another device: no remote copies, remote signals or barrier semaphores. Data moves between devices by JAX's collectives and lax.ppermute only.
A program may use at most 64 MiB of HBM per device.

v0:
```python
import math
import jax
import jax.numpy as jnp
from jax import lax
from jax.sharding import PartitionSpec as P


def positions(block_plan, first_row, row_count, half_rows):
    row_ids = first_row + jnp.arange(row_count, dtype=jnp.int32)
    block_ids = row_ids // half_rows
    block_table = jnp.arange(block_plan.shape[0], dtype=jnp.int32)
    block_start = jnp.sum(
        jnp.where(block_ids[:, None] == block_table[None, :], block_plan[None, :], 0), axis=1
    )
    return block_start * half_rows + row_ids % half_rows


def document_ids(position, doc_ends):
    return jnp.sum((position[:, None] >= doc_ends[None, :]).astype(jnp.int32), axis=1)


def update(state, query_rows, allowed, key_block, value_block, score_scale):
    row_max, row_total, weighted = state
    scores = (
        jnp.einsum("rgd,kd->grk", query_rows, key_block, preferred_element_type=jnp.float32)
        * score_scale
    )
    scores = jnp.where(allowed[None], scores, jnp.float32(-1e30))
    new_max = jnp.maximum(row_max, jnp.max(scores, axis=2))
    weights = jnp.where(allowed[None], jnp.exp(scores - new_max[:, :, None]), jnp.float32(0.0))
    rescale = jnp.exp(row_max - new_max)
    new_total = row_total * rescale + jnp.sum(weights, axis=2)
    probs = weights.astype(jnp.bfloat16)
    new_weighted = weighted * jnp.transpose(rescale)[:, :, None] + jnp.einsum(
        "grk,kd->rgd", probs, value_block, preferred_element_type=jnp.float32
    )
    return (new_max, new_total, new_weighted)


def shards(queries, key_vectors, value_vectors, block_plan, doc_lengths, out_weight):
    span_rows = queries.shape[0]
    half_rows = span_rows // 2
    head_width = key_vectors.shape[1]
    head_count = queries.shape[1] // head_width
    score_scale = 1.0 / math.sqrt(head_width)
    first_row = lax.axis_index("ctx") * span_rows
    doc_ends = jnp.cumsum(doc_lengths)
    query_pos = positions(block_plan, first_row, span_rows, half_rows)
    query_doc = document_ids(query_pos, doc_ends)
    query_heads = queries.reshape(span_rows, head_count, head_width)
    initial = (
        jnp.full((head_count, span_rows), -1e30, jnp.float32),
        jnp.zeros((head_count, span_rows), jnp.float32),
        jnp.zeros((span_rows, head_count, head_width), jnp.float32),
    )
    key_piece = lax.all_gather(key_vectors, "ctx", axis=0, tiled=True)
    value_piece = lax.all_gather(value_vectors, "ctx", axis=0, tiled=True)
    piece_rows = key_piece.shape[0]
    block_rows = math.gcd(piece_rows, span_rows)

    def one_block(block_index, inner):
        offset = block_index * block_rows
        key_block = lax.dynamic_slice_in_dim(key_piece, offset, block_rows, 0)
        value_block = lax.dynamic_slice_in_dim(value_piece, offset, block_rows, 0)
        key_pos = positions(block_plan, offset, block_rows, half_rows)
        key_doc = document_ids(key_pos, doc_ends)
        allowed = (key_pos[None, :] <= query_pos[:, None]) & (
            key_doc[None, :] == query_doc[:, None]
        )
        results = []
        for half_index in range(2):
            low = half_index * half_rows
            high = low + half_rows
            sub_state = (inner[0][:, low:high], inner[1][:, low:high], inner[2][low:high])
            sub_mask = allowed[low:high]
            sub_query = query_heads[low:high]

            def compute(given, sub_query=sub_query, sub_mask=sub_mask):
                return update(given, sub_query, sub_mask, key_block, value_block, score_scale)

            def keep_state(given):
                return given

            results.append(lax.cond(jnp.any(sub_mask), compute, keep_state, sub_state))
        return (
            jnp.concatenate([results[0][0], results[1][0]], axis=1),
            jnp.concatenate([results[0][1], results[1][1]], axis=1),
            jnp.concatenate([results[0][2], results[1][2]], axis=0),
        )

    row_max, row_total, weighted = lax.fori_loop(0, piece_rows // block_rows, one_block, initial)
    attended = (
        (weighted / jnp.transpose(row_total)[:, :, None])
        .reshape(span_rows, head_count * head_width)
        .astype(jnp.bfloat16)
    )
    return jnp.dot(
        attended,
        lax.all_gather(out_weight, "ctx", axis=1, tiled=True),
        preferred_element_type=jnp.float32,
    ).astype(jnp.bfloat16)


def solution(mesh):
    placed = (
        P(("dp", "ctx"), None),
        P(("dp", "ctx"), None),
        P(("dp", "ctx"), None),
        P("dp"),
        P("dp"),
        P(None, "ctx"),
    )
    return jax.shard_map(
        shards, mesh=mesh, in_specs=placed, out_specs=P(("dp", "ctx"), None), check_vma=False
    )
```

profile of v0, /device:TPU:0, one launch (start us, length us, event | category | flops | bytes accessed | tf_op | source)
XLA Modules:
  0.0 117.2 jit_solution(8152489457986995129)
XLA Ops:
  6.5 0.7 all-gather.2.cloned.1.call-update
  7.3 0.7 select_reduce_fusion.1
  8.0 0.8 reduce-window.8
  8.9 1.3 %copy.16 = bf16[512,512]{0,1:T(8,128)(2,1)S(1)} copy(bf16[512,512]{1,0:T(8,128)(2,1)} %param.12) | data formatting | bytes 1048576 | tf_op args[0]
  10.4 22.6 %all_gather.10 = bf16[2048,128]{1,0:T(8,128)(2,1)} all-gather(bf16[512,128]{1,0:T(8,128)(2,1)S(1)} %copy-done), channel_id=1, replica_groups=mesh['dp'=8,'ctx'=4] {'ctx'}, dimensions={0}, use_global_device_ids=true | all-gather | bytes 655360 | tf_op jit(solution)/shard_map/all_gather | solution.py:57
  33.0 22.3 %all_gather.9 = bf16[2048,128]{1,0:T(8,128)(2,1)} all-gather(bf16[512,128]{1,0:T(8,128)(2,1)S(1)} %copy-done.1), channel_id=1, replica_groups=mesh['dp'=8,'ctx'=4] {'ctx'}, dimensions={0}, use_global_device_ids=true | all-gather | bytes 655360 | tf_op jit(solution)/shard_map/all_gather | solution.py:56
  55.4 21.3 %while.19 = (s32[]{:T(128)}, f32[4,512]{1,0:T(4,128)S(1)}, f32[4,512]{1,0:T(4,128)S(1)}, f32[512,4,128]{2,0,1:T(8,128)S(1)}, s32[8]{0:T(128)S(1)}, /*index=5*/s3...) while((s32[]{:T(128)}, f32[4,512]{1,0:T(4,128)S(1)}, ...), condition=%wide.region_16.17_spmd, body=%wide.region_3.16_spmd.sunk | while | flops 552386560 | bytes 22239732 | solution.py:91
  55.9 0.9 slice_reduce_fusion.3
  56.8 1.0 constant_dynamic-slice_fusion.3
  58.5 1.9 %conditional.5 = ((f32[4,256]{1,0:T(4,128)S(1)}, f32[4,256]{1,0:T(4,128)S(1)}, f32[256,4,128]{2,0,1:T(8,128)S(1)})) conditional(s32[]{:T(128)} %convert_element_type.65, (f32[4,256]{1,0:T(4,128)S(1)}, f32[4,256]{1,0:T(4,128)S(1)}, f32[256,4,128]{2,0,1:T(8,128)S(1)}) %tuple.79, (pred[256,512]{0,1:T(8,128)(4,1)S(1)}, ...), branch_computations={%region_7.7_spmd, %region_8.10_spmd} | conditional | flops 275516416 | bytes 8323104 | solution.py:84
  58.6 0.5 fusion
  59.1 0.9 fusion.3
  59.9 0.5 fusion.2
  61.1 1.9 %conditional.4 = ((f32[4,256]{1,0:T(4,128)S(1)}, f32[4,256]{1,0:T(4,128)S(1)}, f32[256,4,128]{2,0,1:T(8,128)S(1)})) conditional(s32[]{:T(128)} %convert_element_type.64, (f32[4,256]{1,0:T(4,128)S(1)}, f32[4,256]{1,0:T(4,128)S(1)}, f32[256,4,128]{2,0,1:T(8,128)S(1)}) %tuple.77, (pred[256,512]{0,1:T(8,128)(4,1)S(1)}, ...), branch_computations={%region_12.12_spmd, %region_13.15_spmd} | conditional | flops 275516416 | bytes 8323104 | solution.py:84
  61.1 0.5 fusion.17
  61.6 0.9 fusion.20
  62.5 0.5 fusion.19
  63.4 0.3 compare_and_fusion.2
  63.7 0.9 slice_reduce_fusion.3
  64.6 1.0 constant_dynamic-slice_fusion.3
  67.3 0.3 compare_and_fusion.2
  67.6 0.9 slice_reduce_fusion.3
  68.4 1.0 constant_dynamic-slice_fusion.3
  70.8 1.9 %conditional.4 = ((f32[4,256]{1,0:T(4,128)S(1)}, f32[4,256]{1,0:T(4,128)S(1)}, f32[256,4,128]{2,0,1:T(8,128)S(1)})) conditional(s32[]{:T(128)} %convert_element_type.64, (f32[4,256]{1,0:T(4,128)S(1)}, f32[4,256]{1,0:T(4,128)S(1)}, f32[256,4,128]{2,0,1:T(8,128)S(1)}) %tuple.77, (pred[256,512]{0,1:T(8,128)(4,1)S(1)}, ...), branch_computations={%region_12.12_spmd, %region_13.15_spmd} | conditional | flops 275516416 | bytes 8323104 | solution.py:84
  70.8 0.5 fusion.17
  71.3 0.9 fusion.20
  72.2 0.5 fusion.19
  73.4 0.9 slice_reduce_fusion.3
  74.2 1.0 constant_dynamic-slice_fusion.3
  76.7 0.3 copy.18
  77.2 26.6 %all-gather.2.cloned.1.call-done = bf16[512,4096]{1,0:T(8,128)(2,1)} async-done(((bf16[512,1024]{1,0:T(8,128)(2,1)}), bf16[512,4096]{1,0:T(8,128)(2,1)}) %all-gather.2.cloned.1.call-update) | async-done | bytes 4194320 | tf_op jit(solution)/shard_map/all_gather | solution.py:99
  103.8 6.6 %convolution_convert_fusion = bf16[512,4096]{1,0:T(8,128)(2,1)} fusion(bf16[512,512]{0,1:T(8,128)(2,1)S(1)} %bitcast.57, bf16[512,4096]{1,0:T(8,128)(2,1)} %all-gather.2.cloned.1.call-done), kind=kOutput, calls=%fused_computation.64 | convolution fusion | flops 2149580800 | bytes 8912896 | tf_op jit(solution)/shard_map/dot_general | solution.py:97
  (67 shorter events, 2.7 us)
Async XLA Ops:
  6.5 3.9 %copy-start = (bf16[512,128]{1,0:T(8,128)(2,1)S(1)}, bf16[512,128]{1,0:T(8,128)(2,1)}, u32[]{:S(2)}) copy-start(bf16[512,128]{1,0:T(8,128)(2,1)} %param.14) | copy-start | bytes 393220
  6.5 26.5 %copy-start.1 = (bf16[512,128]{1,0:T(8,128)(2,1)S(1)}, bf16[512,128]{1,0:T(8,128)(2,1)}, u32[]{:S(2)}) copy-start(bf16[512,128]{1,0:T(8,128)(2,1)} %param.13) | copy-start | bytes 393220
  6.5 97.3 %all-gather.2.cloned.1.call-start = ((), (), s32[]{:S(2)}) async-start(), calls=%async_computation | async-start | bytes 5242880 | tf_op jit(solution)/shard_map/all_gather | solution.py:99
  8.9 46.6 %copy-start.2 = (s32[8]{0:T(128)S(1)}, s32[8]{0:T(128)}, u32[]{:S(2)}) copy-start(s32[8]{0:T(128)} %param.15) | copy-start | bytes 100
Sparse Core Ops, SparseCore 0:
  8.9 94.8 all-gather.1
where the time goes:
time: 118 us; the launch traced here: 117 us
  blocking collectives  44.8 us (38%)
  waiting for transfers between devices  27.3 us (23%)
  between operations  13.5 us (11%)
  matrix products  10.6 us (9%)
  other arithmetic  9.25 us (8%)
  local copies, waits for them, and re-layouts  6.21 us (5%)
  loops' own time  5.56 us (5%)
    all_gather x1, waiting for transfers between devices, shards(): lax.all_gather(out_weight, 'ctx', axis=1, tiled=True)  26.6 us
    all_gather x1, blocking collectives, shards(): value_piece = lax.all_gather(value_vectors, 'ctx', axis=0, tiled=True)  22.6 us
    all_gather x1, blocking collectives, shards(): key_piece = lax.all_gather(key_vectors, 'ctx', axis=0, tiled=True)  22.3 us
    dot_general x1, matrix products, shards(): jnp.dot(attended, lax.all_gather(out_weight, 'ctx', axis=1, tiled=True),...  6.57 us
    another operation x1, loops' own time, shards(): lax.fori_loop(0, piece_rows // block_rows, one_block, initial)  5.42 us
    dynamic_slice x4, local copies, waits for them, and re-layouts, one_block(): key_block = lax.dynamic_slice_in_dim(key_piece, offset, block_rows, 0)  3.96 us
    reduce_or x4, other arithmetic, one_block(): results.append(lax.cond(jnp.any(sub_mask), compute, keep_state, sub_state))  3.53 us
    dot_general x3, matrix products, update(): jnp.einsum('grk,kd->rgd', probs, value_block, preferred_element_type=jnp....  2.59 us
  transfers between devices with their start and end apart: 1, of which 1 were waited for; matrix products, arithmetic and copies ran while one was open for 17% of the time, Pallas kernels for 0%

commit v1 on v0

--- a/solution.py
+++ b/solution.py
@@ -3,6 +3,7 @@
 import jax.numpy as jnp
 from jax import lax
 from jax.sharding import PartitionSpec as P
+from jax.lax import all_gather
 
 
 def positions(block_plan, first_row, row_count, half_rows):
@@ -53,8 +54,15 @@
         jnp.zeros((head_count, span_rows), jnp.float32),
         jnp.zeros((span_rows, head_count, head_width), jnp.float32),
     )
-    key_piece = lax.all_gather(key_vectors, "ctx", axis=0, tiled=True)
-    value_piece = lax.all_gather(value_vectors, "ctx", axis=0, tiled=True)
+
+    def keys_render(view, load):
+        return jnp.split(
+            all_gather(jnp.concatenate([view, load], 1), "ctx", axis=0, tiled=True),
+            [view.shape[1]],
+            1,
+        )
+
+    key_piece, value_piece = keys_render(key_vectors, value_vectors)
     piece_rows = key_piece.shape[0]
     block_rows = math.gcd(piece_rows, span_rows)
 

time: 118 us -> 135 us (1.14)
  waiting for transfers between devices: 27.3 us -> 86.9 us
  blocking collectives: 44.8 us -> 0 us
  other arithmetic: 9.25 us -> 10.9 us
    all_gather x2 -> x0, blocking collectives: 44.8 us -> none  [the longest x1 22.6 us: shards(): value_piece = lax.all_gather(value_vectors, 'ctx', axis=0, tiled=True)]
    all_gather x1, waiting for transfers between devices: 26.6 us -> 57.8 us  [shards(): lax.all_gather(out_weight, 'ctx', axis=1, tiled=True)]
    all_gather x0 -> x1, waiting for transfers between devices: none -> 28.4 us  [keys_render(): all_gather(jnp.concatenate([view, load], 1), 'ctx', axis=0, tiled=True)]
    split x0 -> x1, local copies, waits for them, and re-layouts: none -> 2.25 us  [keys_render(): jnp.split(all_gather(jnp.concatenate([view, load], 1), 'ctx', axis=0, til...]
    concatenate x0 -> x1, other arithmetic: none -> 1.76 us  [keys_render(): jnp.concatenate([view, load], 1)]
  transfers between devices with their start and end apart: 1 -> 2, of which waited for: 1 -> 2; matrix products, arithmetic and copies ran while one was open for 17% -> 15% of each run, Pallas kernels for 0% -> 0%
where the time goes in v1:
time: 135 us
  waiting for transfers between devices  86.9 us (64%)
  between operations  13.5 us (10%)
  other arithmetic  10.9 us (8%)
  matrix products  10.6 us (8%)
  local copies, waits for them, and re-layouts  7.4 us (5%)
  loops' own time  5.4 us (4%)
    all_gather x1, waiting for transfers between devices, shards(): lax.all_gather(out_weight, 'ctx', axis=1, tiled=True)  57.8 us
    all_gather x1, waiting for transfers between devices, keys_render(): all_gather(jnp.concatenate([view, load], 1), 'ctx', axis=0, tiled=True)  28.4 us
    dot_general x1, matrix products, shards(): jnp.dot(attended, lax.all_gather(out_weight, 'ctx', axis=1, tiled=True),...  6.57 us
    another operation x1, loops' own time, shards(): lax.fori_loop(0, piece_rows // block_rows, one_block, initial)  5.26 us
    dynamic_slice x4, local copies, waits for them, and re-layouts, one_block(): key_block = lax.dynamic_slice_in_dim(key_piece, offset, block_rows, 0)  3.95 us
    reduce_or x4, other arithmetic, one_block(): results.append(lax.cond(jnp.any(sub_mask), compute, keep_state, sub_state))  3.4 us
  transfers between devices with their start and end apart: 2, of which 2 were waited for; matrix products, arithmetic and copies ran while one was open for 15% of the time, Pallas kernels for 0%

profile of v1, /device:TPU:0, one launch (start us, length us, event | category | flops | bytes accessed | tf_op | source)
XLA Modules:
  0.0 134.8 jit_solution(15466205037087640618)
XLA Ops:
  6.5 1.8 %pad_maximum_fusion.3 = bf16[512,256]{1,0:T(8,128)(2,1)} fusion(bf16[512,128]{1,0:T(8,128)(2,1)} %param.14, bf16[512,128]{1,0:T(8,128)(2,1)} %param.13), kind=kLoop, calls=%fused_computation.66 | loop fusion | flops 524288 | bytes 524288 | tf_op jit(solution)/shard_map/concatenate | solution.py:60
  8.4 0.7 all-gather.5.cloned.1.call-update
  9.1 0.7 select_reduce_fusion.1
  9.9 0.8 reduce-window.8
  11.3 28.4 %all-gather.3.cloned.1.call-done = bf16[2048,256]{1,0:T(8,128)(2,1)} async-done(((bf16[512,256]{1,0:T(8,128)(2,1)}), bf16[2048,256]{1,0:T(8,128)(2,1)}) %all-gather.3.cloned.1.call-update) | async-done | bytes 1048592 | tf_op jit(solution)/shard_map/all_gather | solution.py:60
  39.6 2.2 %fusion.45 = (bf16[2048,128]{1,0:T(8,128)(2,1)}, bf16[2048,128]{1,0:T(8,128)(2,1)}) fusion(bf16[2048,256]{1,0:T(8,128)(2,1)} %all-gather.3.cloned.1.call-done), kind=kLoop, calls=%fused_computation.84 | loop fusion | bytes 2097152 | tf_op jit(solution)/shard_map/split | solution.py:59
  42.0 21.0 %while.19 = (s32[]{:T(128)}, f32[4,512]{1,0:T(4,128)S(1)}, f32[4,512]{1,0:T(4,128)S(1)}, f32[512,4,128]{2,0,1:T(8,128)S(1)}, s32[8]{0:T(128)S(1)}, /*index=5*/s3...) while((s32[]{:T(128)}, f32[4,512]{1,0:T(4,128)S(1)}, ...), condition=%wide.region_16.17_spmd, body=%wide.region_3.16_spmd.sunk | while | flops 552386560 | bytes 22239732 | solution.py:99
  42.2 0.3 compare_and_fusion.2
  42.5 0.8 slice_reduce_fusion.3
  43.3 1.0 constant_dynamic-slice_fusion.3
  45.0 2.0 %conditional.5 = ((f32[4,256]{1,0:T(4,128)S(1)}, f32[4,256]{1,0:T(4,128)S(1)}, f32[256,4,128]{2,0,1:T(8,128)S(1)})) conditional(s32[]{:T(128)} %convert_element_type.65, (f32[4,256]{1,0:T(4,128)S(1)}, f32[4,256]{1,0:T(4,128)S(1)}, f32[256,4,128]{2,0,1:T(8,128)S(1)}) %tuple.80, (pred[256,512]{0,1:T(8,128)(4,1)S(1)}, ...), branch_computations={%region_7.7_spmd, %region_8.10_spmd} | conditional | flops 275516416 | bytes 8323104 | solution.py:92
  45.1 0.5 fusion
  45.6 0.9 fusion.3
  46.4 0.5 fusion.2
  47.6 1.9 %conditional.4 = ((f32[4,256]{1,0:T(4,128)S(1)}, f32[4,256]{1,0:T(4,128)S(1)}, f32[256,4,128]{2,0,1:T(8,128)S(1)})) conditional(s32[]{:T(128)} %convert_element_type.64, (f32[4,256]{1,0:T(4,128)S(1)}, f32[4,256]{1,0:T(4,128)S(1)}, f32[256,4,128]{2,0,1:T(8,128)S(1)}) %tuple.78, (pred[256,512]{0,1:T(8,128)(4,1)S(1)}, ...), branch_computations={%region_12.12_spmd, %region_13.15_spmd} | conditional | flops 275516416 | bytes 8323104 | solution.py:92
  47.6 0.5 fusion.17
  48.1 0.9 fusion.20
  49.0 0.5 fusion.19
  49.9 0.3 compare_and_fusion.2
  50.2 0.8 slice_reduce_fusion.3
  51.0 1.0 constant_dynamic-slice_fusion.3
  54.0 0.8 slice_reduce_fusion.3
  54.8 1.0 constant_dynamic-slice_fusion.3
  57.2 2.0 %conditional.4 = ((f32[4,256]{1,0:T(4,128)S(1)}, f32[4,256]{1,0:T(4,128)S(1)}, f32[256,4,128]{2,0,1:T(8,128)S(1)})) conditional(s32[]{:T(128)} %convert_element_type.64, (f32[4,256]{1,0:T(4,128)S(1)}, f32[4,256]{1,0:T(4,128)S(1)}, f32[256,4,128]{2,0,1:T(8,128)S(1)}) %tuple.78, (pred[256,512]{0,1:T(8,128)(4,1)S(1)}, ...), branch_computations={%region_12.12_spmd, %region_13.15_spmd} | conditional | flops 275516416 | bytes 8323104 | solution.py:92
  57.2 0.5 fusion.17
  57.7 0.9 fusion.20
  58.6 0.5 fusion.19
  59.7 0.8 slice_reduce_fusion.3
  60.6 1.0 constant_dynamic-slice_fusion.3
  63.0 0.3 copy.18
  63.5 57.8 %all-gather.5.cloned.1.call-done = bf16[512,4096]{1,0:T(8,128)(2,1)} async-done(((bf16[512,1024]{1,0:T(8,128)(2,1)}), bf16[512,4096]{1,0:T(8,128)(2,1)}) %all-gather.5.cloned.1.call-update) | async-done | bytes 4194320 | tf_op jit(solution)/shard_map/all_gather | solution.py:107
  121.4 6.6 %convolution_convert_fusion = bf16[512,4096]{1,0:T(8,128)(2,1)} fusion(bf16[512,512]{0,1:T(8,128)(2,1)S(1)} %bitcast.57, bf16[512,4096]{1,0:T(8,128)(2,1)} %all-gather.5.cloned.1.call-done), kind=kOutput, calls=%fused_computation.64 | convolution fusion | flops 2149580800 | bytes 8912896 | tf_op jit(solution)/shard_map/dot_general | solution.py:105
  (68 shorter events, 3.0 us)
Async XLA Ops:
  6.5 4.1 %copy-start = (bf16[512,512]{1,0:T(8,128)(2,1)S(1)}, bf16[512,512]{1,0:T(8,128)(2,1)}, u32[]{:S(2)}) copy-start(bf16[512,512]{1,0:T(8,128)(2,1)} %param.12) | copy-start | bytes 1572868
  6.5 33.1 %all-gather.3.cloned.1.call-start = ((), (), s32[]{:S(2)}) async-start(), calls=%async_computation | async-start | bytes 1310720 | tf_op jit(solution)/shard_map/all_gather | solution.py:60
  8.3 113.0 %all-gather.5.cloned.1.call-start = ((), (), s32[]{:S(2)}) async-start(), calls=%async_computation.1 | async-start | bytes 5242880 | tf_op jit(solution)/shard_map/all_gather | solution.py:107
  10.9 31.1 %copy-start.1 = (s32[8]{0:T(128)S(1)}, s32[8]{0:T(128)}, u32[]{:S(2)}) copy-start(s32[8]{0:T(128)} %param.15) | copy-start | bytes 100
Sparse Core Ops, SparseCore 0:
  8.9 30.6 all-gather.2
  41.2 80.1 all-gather.4
